TPU v7x, 256 devices: a whole 4x4x8 slice. The times are simulated.
256 devices in a mesh: segment: 4 (over x), space: 64 (over z, y, core).
Axes of the slice: x: 4, y: 4, z: 8, core: 2. Of those that a mesh axis runs over, the one named last changes fastest.
Arguments:
- frames: bfloat16 [4, 1024, 32, 64], P(None, 'space'), may hold values from -6 to 6
- hidden_prev: bfloat16 [4, 4, 1024, 32, 128], P('segment', None, 'space'), may hold values from -1 to 1
- cell_prev: float32 [4, 4, 1024, 32, 128], P('segment', None, 'space'), may hold values from -6 to 6
- kernels: bfloat16 [4, 5, 5, 256, 512], P('segment'), may hold values from -0.078125 to 0.078125
- biases: float32 [4, 512], P('segment'), may hold values from -4 to 4
Outputs:
- hidden_next: bfloat16 [4, 4, 1024, 32, 128], P('segment', None, 'space')
- cell_next: float32 [4, 4, 1024, 32, 128], P('segment', None, 'space')
All inputs are finite; a program needn't handle non-finite values.
Results may differ from a plain program's by a relative error of at most 0.0095.
Values may be sent and summed in bfloat16 or wider, within the bound.
A program may use at most 128 MiB of HBM per device.

v0:
```python
from functools import partial

import jax
import jax.numpy as jnp
from jax import lax
from jax.sharding import PartitionSpec as P


def with_halo(x, sides, width):
    for axis, dim in sides:
        count, length = (lax.axis_size(axis), x.shape[dim])
        up = [(i, (i + 1) % count) for i in range(count - 1)]
        down = [(j, i) for i, j in up]
        last = lax.slice_in_dim(x, length - width, length, axis=dim)
        initial = lax.slice_in_dim(x, 0, width, axis=dim)
        before = lax.ppermute(last, axis, up)
        after = lax.ppermute(initial, axis, down)
        x = jnp.concatenate([before, x, after], axis=dim)
    return x


def shortened(x):
    return jax.tree.map(lambda a: a.astype(jnp.bfloat16) if a.dtype == jnp.float32 else a, x)


def shifted(x, axis, by):
    count = lax.axis_size(axis)
    pairs = [(i, i + by) for i in range(count) if 0 <= i + by < count]
    return lax.ppermute(x, axis, pairs)


def layer_kernel(kernel, inputs_width, hidden_width, wide):
    rows_cut = jnp.concatenate(
        [kernel[:, :, 0:inputs_width], kernel[:, :, wide : wide + hidden_width]], axis=2
    )
    return jnp.concatenate(
        [rows_cut[..., k * wide : k * wide + hidden_width] for k in range(4)], axis=-1
    )


def layer_bias(bias, hidden_width, wide):
    return jnp.concatenate([bias[k * wide : k * wide + hidden_width] for k in range(4)], axis=-1)


def cell_update(padded, kernel, bias, cell_old):
    rows = padded.shape[0] - 4
    cols = padded.shape[1]
    hid = cell_old.shape[-1]
    broad = jnp.pad(padded, ((0, 0), (2, 2), (0, 0)))
    windows = [
        broad[first : first + rows, second : second + cols, :]
        for first in range(5)
        for second in range(5)
    ]
    patches = jnp.concatenate(windows, axis=-1).reshape(rows * cols, -1)
    flat_kernel = kernel.reshape(-1, kernel.shape[-1])
    gates = jnp.dot(patches, flat_kernel, preferred_element_type=jnp.float32) + bias
    gates = gates.reshape(rows, cols, -1)
    gate_in = jax.nn.sigmoid(gates[..., 0:hid])
    gate_forget = jax.nn.sigmoid(gates[..., hid : 2 * hid])
    candidate = jnp.tanh(gates[..., 2 * hid : 3 * hid])
    gate_out = jax.nn.sigmoid(gates[..., 3 * hid : 4 * hid])
    cell_new = gate_forget * cell_old + gate_in * candidate
    hidden_new = (gate_out * jnp.tanh(cell_new)).astype(jnp.bfloat16)
    return (hidden_new, cell_new)


def layer_step(padded, kernel, bias, cell_old, inputs_width, hidden_width):
    wide = cell_old.shape[-1]
    joined = jnp.concatenate(
        [padded[..., 0:inputs_width], padded[..., wide : wide + hidden_width]], axis=-1
    )
    hidden_new, cell_new = cell_update(
        joined,
        layer_kernel(kernel, inputs_width, hidden_width, wide),
        layer_bias(bias, hidden_width, wide),
        cell_old[..., 0:hidden_width],
    )
    widen = ((0, 0), (0, 0), (0, wide - hidden_width))
    return (jnp.pad(hidden_new, widen), jnp.pad(cell_new, widen))


def spare_step(padded, kernel, bias, cell_old):
    return (jnp.zeros(cell_old.shape, jnp.bfloat16), jnp.zeros_like(cell_old))


def on_device(frames, hidden_prev, cell_prev, kernels, biases):
    segments = lax.axis_size("segment")
    position = lax.axis_index("segment")
    batches = frames.shape[0]
    narrow = frames.shape[-1]
    wide = hidden_prev.shape[-1]
    hidden_widths = [narrow, wide, wide, narrow]
    input_widths = [narrow, narrow, wide, wide]
    frames_wide = jnp.pad(frames, ((0, 0), (0, 0), (0, 0), (0, wide - narrow)))
    kernel = kernels[0]
    bias = biases[0]
    ticks = batches + segments - 1
    branches = [
        partial(layer_step, inputs_width=input_widths[k], hidden_width=hidden_widths[k])
        for k in range(segments)
    ]
    branches.append(spare_step)

    def tick(step, carry):
        incoming, hidden_out, cell_out = carry
        batch = step - position
        active = jnp.logical_and(batch >= 0, batch < batches)
        index = jnp.clip(batch, 0, batches - 1)
        frame_now = lax.dynamic_index_in_dim(frames_wide, index, 0, keepdims=False)
        layer_input = jnp.where(position == 0, frame_now, incoming)
        state_now = lax.dynamic_index_in_dim(hidden_prev[0], index, 0, keepdims=False)
        joined = jnp.concatenate([layer_input, state_now], axis=-1)
        padded = with_halo(joined, (("space", 0),), 2)
        cell_old = lax.dynamic_index_in_dim(cell_prev[0], index, 0, keepdims=False)
        which = jnp.where(active, position, segments)
        hidden_new, cell_new = lax.switch(which, branches, padded, kernel, bias, cell_old)
        kept_hidden = lax.dynamic_index_in_dim(hidden_out, index, 0, keepdims=False)
        kept_cell = lax.dynamic_index_in_dim(cell_out, index, 0, keepdims=False)
        hidden_out = lax.dynamic_update_index_in_dim(
            hidden_out, jnp.where(active, hidden_new, kept_hidden), index, 0
        )
        cell_out = lax.dynamic_update_index_in_dim(
            cell_out, jnp.where(active, cell_new, kept_cell), index, 0
        )
        passed = jax.tree.map(
            lambda part, own: part.astype(own.dtype),
            shifted(shortened(hidden_new), "segment", 1),
            hidden_new,
        )
        return (passed, hidden_out, cell_out)

    start = (
        jnp.zeros_like(frames_wide[0]),
        jnp.zeros_like(hidden_prev[0]),
        jnp.zeros_like(cell_prev[0]),
    )
    final = lax.fori_loop(0, ticks, tick, start)
    return (final[1][None], final[2][None])


def solution(mesh):
    return jax.shard_map(
        on_device,
        mesh=mesh,
        in_specs=(
            P(None, "space", None, None),
            P("segment", None, "space", None, None),
            P("segment", None, "space", None, None),
            P("segment", None, None, None, None),
            P("segment", None),
        ),
        out_specs=(
            P("segment", None, "space", None, None),
            P("segment", None, "space", None, None),
        ),
        check_vma=False,
    )
```

profile of v0, /device:TPU:134, one launch (start us, length us, event | category | flops | bytes accessed | tf_op | source)
XLA Modules:
  0.0 265.6 jit_solution(17780078874064567434)
XLA Ops:
  0.6 2.0 pad.41
  5.3 260.3 %while.18 = (s32[]{:T(128)}, bf16[16,32,128]{2,1,0:T(8,128)(2,1)}, bf16[4,16,32,128]{3,2,1,0:T(8,128)(2,1)}, f32[4,16,32,128]{3,2,1,0:T(8,128)}, s32[]{:T(128)},...) while((s32[]{:T(128)}, bf16[16,32,128]{2,1,0:T(8,128)(2,1)}, ...), condition=%wide.region_6.7_spmd, body=%wide.region_0.6_spmd.sunk | while | flops 3358261248 | bytes 68054512 | solution.py:138
  7.2 3.9 %collective-permute-start = (bf16[2,32,256]{2,1,0:T(8,128)(2,1)S(1)}, bf16[2,32,256]{2,1,0:T(8,128)(2,1)S(1)}, u32[]{:S(2)}, u32[]{:S(2)}) collective-permute-start(bf16[2,32,256]{2,1,0:T(8,128)(2,1)S(1)} %get-tuple-element.505), channel_id=1, source_target_pairs={{1,0},{2,1},{3,2},{4,3},{5,4},{6,5},{7,6},{8,7},{9,8},{10,9},{11,1... | collective-permute-start | bytes 98312 | tf_op jit(solution)/shard_map/while/body/eval_jaxpr/ppermute | solution.py:17
  11.1 1.9 collective-permute-start.1
  15.0 4.7 %collective-permute-done.1 = bf16[2,32,256]{2,1,0:T(8,128)(2,1)S(1)} collective-permute-done((bf16[2,32,256]{2,1,0:T(8,128)(2,1)S(1)}, bf16[2,32,256]{2,1,0:T(8,128)(2,1)S(1)}, u32[]{:S(2)}, u32[]{:S(2)}) %collective-permute-start.1) | collective-permute-done | bytes 32800 | tf_op jit(solution)/shard_map/while/body/eval_jaxpr/ppermute | solution.py:16
  22.5 4.2 %collective-permute-done.2 = bf16[16,32,128]{2,1,0:T(8,128)(2,1)} collective-permute-done((bf16[16,32,128]{2,1,0:T(8,128)(2,1)S(1)}, bf16[16,32,128]{2,1,0:T(8,128)(2,1)}, u32[]{:S(2)}, u32[]{:S(2)}) %collective-permute-start.2) | collective-permute-done | bytes 131104 | tf_op jit(solution)/shard_map/while/body/eval_jaxpr/ppermute | solution.py:29
  28.7 1.9 collective-permute-start
  30.6 2.4 collective-permute-start.1
  35.0 4.2 %collective-permute-done.1 = bf16[2,32,256]{2,1,0:T(8,128)(2,1)S(1)} collective-permute-done((bf16[2,32,256]{2,1,0:T(8,128)(2,1)S(1)}, bf16[2,32,256]{2,1,0:T(8,128)(2,1)S(1)}, u32[]{:S(2)}, u32[]{:S(2)}) %collective-permute-start.1) | collective-permute-done | bytes 32800 | tf_op jit(solution)/shard_map/while/body/eval_jaxpr/ppermute | solution.py:16
  42.1 4.2 %collective-permute-done.2 = bf16[16,32,128]{2,1,0:T(8,128)(2,1)} collective-permute-done((bf16[16,32,128]{2,1,0:T(8,128)(2,1)S(1)}, bf16[16,32,128]{2,1,0:T(8,128)(2,1)}, u32[]{:S(2)}, u32[]{:S(2)}) %collective-permute-start.2) | collective-permute-done | bytes 131104 | tf_op jit(solution)/shard_map/while/body/eval_jaxpr/ppermute | solution.py:29
  48.2 1.9 collective-permute-start
  50.2 2.4 collective-permute-start.1
  54.5 4.2 %collective-permute-done.1 = bf16[2,32,256]{2,1,0:T(8,128)(2,1)S(1)} collective-permute-done((bf16[2,32,256]{2,1,0:T(8,128)(2,1)S(1)}, bf16[2,32,256]{2,1,0:T(8,128)(2,1)S(1)}, u32[]{:S(2)}, u32[]{:S(2)}) %collective-permute-start.1) | collective-permute-done | bytes 32800 | tf_op jit(solution)/shard_map/while/body/eval_jaxpr/ppermute | solution.py:16
  61.6 38.4 %collective-permute-done.2 = bf16[16,32,128]{2,1,0:T(8,128)(2,1)} collective-permute-done((bf16[16,32,128]{2,1,0:T(8,128)(2,1)S(1)}, bf16[16,32,128]{2,1,0:T(8,128)(2,1)}, u32[]{:S(2)}, u32[]{:S(2)}) %collective-permute-start.2) | collective-permute-done | bytes 131104 | tf_op jit(solution)/shard_map/while/body/eval_jaxpr/ppermute | solution.py:29
  101.9 1.9 collective-permute-start
  103.8 2.4 collective-permute-start.1
  108.2 4.2 %collective-permute-done.1 = bf16[2,32,256]{2,1,0:T(8,128)(2,1)S(1)} collective-permute-done((bf16[2,32,256]{2,1,0:T(8,128)(2,1)S(1)}, bf16[2,32,256]{2,1,0:T(8,128)(2,1)S(1)}, u32[]{:S(2)}, u32[]{:S(2)}) %collective-permute-start.1) | collective-permute-done | bytes 32800 | tf_op jit(solution)/shard_map/while/body/eval_jaxpr/ppermute | solution.py:16
  112.4 20.7 %conditional.2 = ((bf16[16,32,128]{2,1,0:T(8,128)(2,1)S(1)}, f32[16,32,128]{2,1,0:T(8,128)S(1)})) conditional(s32[]{:T(128)} %clamp.9, (bf16[20,32,256]{2,1,0:T(8,128)(2,1)S(1)}, bf16[5,5,256,512]{3,2,1,0:T(8,128)(2,1)}, f32[512]{0:T(512)}, f32[1,4,16,32,128]{4,3,2,1,0:T(8,128)}, s32[]{:T(128)}) %tuple.132, ...), branch_computations={%region_1.1_spmd, %region_2.2_spmd, %region_3.3_spmd, %region_4.4_... | conditional | flops 3356622848 | bytes 63662168 | solution.py:117
  112.5 2.3 pad_slice_fusion.76
  115.0 10.0 %concatenate.73 = bf16[16,32,4800]{2,1,0:T(8,128)(2,1)} concatenate(bf16[16,32,192]{2,1,0:T(8,128)(2,1)S(1)} %get-tuple-element.431, bf16[16,32,192]{2,1,0:T(8,128)(2,1)S(1)} %get-tuple-element.404, bf16[16,32,192]{2,1,0:T(8,128)(2,1)S(1)} %get-tuple-element.426, bf16[16,32,192]{2,1,0:T(8,128)(2,1)S(1)} %get-tuple-element.405, bf16[16,32,192]{2,1,0:T(8,128)(2,1)S(1)} %get-tuple-element.406, ...), dimensions={2} | concatenate | bytes 9830400 | tf_op jit(solution)/shard_map/while/body/eval_jaxpr/cond/branch_3_fun/concatenate | solution.py:55
  125.0 2.8 %fusion.113 = (bf16[5,5,192,64]{3,2,1,0:T(8,128)(2,1)S(1)}, bf16[5,5,192,64]{3,2,1,0:T(8,128)(2,1)S(1)}, bf16[5,5,192,64]{3,2,1,0:T(8,128)(2,1)S(1)}, bf16[5,5,192,64]{3,2,1,0:T(8,128)(2,1)S(1)}) fusion(bf16[5,5,256,512]{3,2,1,0:T(8,128)(2,1)} %get-tuple-element.309), kind=kLoop, calls=%fused_computation.257 | loop fusion | bytes 4915200 | tf_op jit(solution)/shard_map/while/body/eval_jaxpr/cond/branch_3_fun/slice | solution.py:37
  127.9 1.7 pad_maximum_fusion.4
  135.8 6.0 %collective-permute-done.2 = bf16[16,32,128]{2,1,0:T(8,128)(2,1)} collective-permute-done((bf16[16,32,128]{2,1,0:T(8,128)(2,1)S(1)}, bf16[16,32,128]{2,1,0:T(8,128)(2,1)}, u32[]{:S(2)}, u32[]{:S(2)}) %collective-permute-start.2) | collective-permute-done | bytes 131104 | tf_op jit(solution)/shard_map/while/body/eval_jaxpr/ppermute | solution.py:29
  143.8 1.9 collective-permute-start
  145.7 2.4 collective-permute-start.1
  150.0 4.2 %collective-permute-done.1 = bf16[2,32,256]{2,1,0:T(8,128)(2,1)S(1)} collective-permute-done((bf16[2,32,256]{2,1,0:T(8,128)(2,1)S(1)}, bf16[2,32,256]{2,1,0:T(8,128)(2,1)S(1)}, u32[]{:S(2)}, u32[]{:S(2)}) %collective-permute-start.1) | collective-permute-done | bytes 32800 | tf_op jit(solution)/shard_map/while/body/eval_jaxpr/ppermute | solution.py:16
  154.3 20.7 %conditional.2 = ((bf16[16,32,128]{2,1,0:T(8,128)(2,1)S(1)}, f32[16,32,128]{2,1,0:T(8,128)S(1)})) conditional(s32[]{:T(128)} %clamp.9, (bf16[20,32,256]{2,1,0:T(8,128)(2,1)S(1)}, bf16[5,5,256,512]{3,2,1,0:T(8,128)(2,1)}, f32[512]{0:T(512)}, f32[1,4,16,32,128]{4,3,2,1,0:T(8,128)}, s32[]{:T(128)}) %tuple.132, ...), branch_computations={%region_1.1_spmd, %region_2.2_spmd, %region_3.3_spmd, %region_4.4_... | conditional | flops 3356622848 | bytes 63662168 | solution.py:117
  154.3 2.3 pad_slice_fusion.76
  156.8 10.0 %concatenate.73 = bf16[16,32,4800]{2,1,0:T(8,128)(2,1)} concatenate(bf16[16,32,192]{2,1,0:T(8,128)(2,1)S(1)} %get-tuple-element.431, bf16[16,32,192]{2,1,0:T(8,128)(2,1)S(1)} %get-tuple-element.404, bf16[16,32,192]{2,1,0:T(8,128)(2,1)S(1)} %get-tuple-element.426, bf16[16,32,192]{2,1,0:T(8,128)(2,1)S(1)} %get-tuple-element.405, bf16[16,32,192]{2,1,0:T(8,128)(2,1)S(1)} %get-tuple-element.406, ...), dimensions={2} | concatenate | bytes 9830400 | tf_op jit(solution)/shard_map/while/body/eval_jaxpr/cond/branch_3_fun/concatenate | solution.py:55
  166.9 2.8 %fusion.113 = (bf16[5,5,192,64]{3,2,1,0:T(8,128)(2,1)S(1)}, bf16[5,5,192,64]{3,2,1,0:T(8,128)(2,1)S(1)}, bf16[5,5,192,64]{3,2,1,0:T(8,128)(2,1)S(1)}, bf16[5,5,192,64]{3,2,1,0:T(8,128)(2,1)S(1)}) fusion(bf16[5,5,256,512]{3,2,1,0:T(8,128)(2,1)} %get-tuple-element.309), kind=kLoop, calls=%fused_computation.257 | loop fusion | bytes 4915200 | tf_op jit(solution)/shard_map/while/body/eval_jaxpr/cond/branch_3_fun/slice | solution.py:37
  169.7 1.7 pad_maximum_fusion.4
  177.7 6.0 %collective-permute-done.2 = bf16[16,32,128]{2,1,0:T(8,128)(2,1)} collective-permute-done((bf16[16,32,128]{2,1,0:T(8,128)(2,1)S(1)}, bf16[16,32,128]{2,1,0:T(8,128)(2,1)}, u32[]{:S(2)}, u32[]{:S(2)}) %collective-permute-start.2) | collective-permute-done | bytes 131104 | tf_op jit(solution)/shard_map/while/body/eval_jaxpr/ppermute | solution.py:29
  185.6 1.9 collective-permute-start
  187.5 2.4 collective-permute-start.1
  191.9 4.2 %collective-permute-done.1 = bf16[2,32,256]{2,1,0:T(8,128)(2,1)S(1)} collective-permute-done((bf16[2,32,256]{2,1,0:T(8,128)(2,1)S(1)}, bf16[2,32,256]{2,1,0:T(8,128)(2,1)S(1)}, u32[]{:S(2)}, u32[]{:S(2)}) %collective-permute-start.1) | collective-permute-done | bytes 32800 | tf_op jit(solution)/shard_map/while/body/eval_jaxpr/ppermute | solution.py:16
  196.1 20.7 %conditional.2 = ((bf16[16,32,128]{2,1,0:T(8,128)(2,1)S(1)}, f32[16,32,128]{2,1,0:T(8,128)S(1)})) conditional(s32[]{:T(128)} %clamp.9, (bf16[20,32,256]{2,1,0:T(8,128)(2,1)S(1)}, bf16[5,5,256,512]{3,2,1,0:T(8,128)(2,1)}, f32[512]{0:T(512)}, f32[1,4,16,32,128]{4,3,2,1,0:T(8,128)}, s32[]{:T(128)}) %tuple.132, ...), branch_computations={%region_1.1_spmd, %region_2.2_spmd, %region_3.3_spmd, %region_4.4_... | conditional | flops 3356622848 | bytes 63662168 | solution.py:117
  196.2 2.3 pad_slice_fusion.76
  198.7 10.0 %concatenate.73 = bf16[16,32,4800]{2,1,0:T(8,128)(2,1)} concatenate(bf16[16,32,192]{2,1,0:T(8,128)(2,1)S(1)} %get-tuple-element.431, bf16[16,32,192]{2,1,0:T(8,128)(2,1)S(1)} %get-tuple-element.404, bf16[16,32,192]{2,1,0:T(8,128)(2,1)S(1)} %get-tuple-element.426, bf16[16,32,192]{2,1,0:T(8,128)(2,1)S(1)} %get-tuple-element.405, bf16[16,32,192]{2,1,0:T(8,128)(2,1)S(1)} %get-tuple-element.406, ...), dimensions={2} | concatenate | bytes 9830400 | tf_op jit(solution)/shard_map/while/body/eval_jaxpr/cond/branch_3_fun/concatenate | solution.py:55
  208.7 2.8 %fusion.113 = (bf16[5,5,192,64]{3,2,1,0:T(8,128)(2,1)S(1)}, bf16[5,5,192,64]{3,2,1,0:T(8,128)(2,1)S(1)}, bf16[5,5,192,64]{3,2,1,0:T(8,128)(2,1)S(1)}, bf16[5,5,192,64]{3,2,1,0:T(8,128)(2,1)S(1)}) fusion(bf16[5,5,256,512]{3,2,1,0:T(8,128)(2,1)} %get-tuple-element.309), kind=kLoop, calls=%fused_computation.257 | loop fusion | bytes 4915200 | tf_op jit(solution)/shard_map/while/body/eval_jaxpr/cond/branch_3_fun/slice | solution.py:37
  219.5 6.0 %collective-permute-done.2 = bf16[16,32,128]{2,1,0:T(8,128)(2,1)} collective-permute-done((bf16[16,32,128]{2,1,0:T(8,128)(2,1)S(1)}, bf16[16,32,128]{2,1,0:T(8,128)(2,1)}, u32[]{:S(2)}, u32[]{:S(2)}) %collective-permute-start.2) | collective-permute-done | bytes 131104 | tf_op jit(solution)/shard_map/while/body/eval_jaxpr/ppermute | solution.py:29
  227.5 1.9 collective-permute-start
  229.4 2.4 collective-permute-start.1
  233.7 4.2 %collective-permute-done.1 = bf16[2,32,256]{2,1,0:T(8,128)(2,1)S(1)} collective-permute-done((bf16[2,32,256]{2,1,0:T(8,128)(2,1)S(1)}, bf16[2,32,256]{2,1,0:T(8,128)(2,1)S(1)}, u32[]{:S(2)}, u32[]{:S(2)}) %collective-permute-start.1) | collective-permute-done | bytes 32800 | tf_op jit(solution)/shard_map/while/body/eval_jaxpr/ppermute | solution.py:16
  238.0 20.7 %conditional.2 = ((bf16[16,32,128]{2,1,0:T(8,128)(2,1)S(1)}, f32[16,32,128]{2,1,0:T(8,128)S(1)})) conditional(s32[]{:T(128)} %clamp.9, (bf16[20,32,256]{2,1,0:T(8,128)(2,1)S(1)}, bf16[5,5,256,512]{3,2,1,0:T(8,128)(2,1)}, f32[512]{0:T(512)}, f32[1,4,16,32,128]{4,3,2,1,0:T(8,128)}, s32[]{:T(128)}) %tuple.132, ...), branch_computations={%region_1.1_spmd, %region_2.2_spmd, %region_3.3_spmd, %region_4.4_... | conditional | flops 3356622848 | bytes 63662168 | solution.py:117
  238.0 2.3 pad_slice_fusion.76
  240.5 10.0 %concatenate.73 = bf16[16,32,4800]{2,1,0:T(8,128)(2,1)} concatenate(bf16[16,32,192]{2,1,0:T(8,128)(2,1)S(1)} %get-tuple-element.431, bf16[16,32,192]{2,1,0:T(8,128)(2,1)S(1)} %get-tuple-element.404, bf16[16,32,192]{2,1,0:T(8,128)(2,1)S(1)} %get-tuple-element.426, bf16[16,32,192]{2,1,0:T(8,128)(2,1)S(1)} %get-tuple-element.405, bf16[16,32,192]{2,1,0:T(8,128)(2,1)S(1)} %get-tuple-element.406, ...), dimensions={2} | concatenate | bytes 9830400 | tf_op jit(solution)/shard_map/while/body/eval_jaxpr/cond/branch_3_fun/concatenate | solution.py:55
  250.6 2.8 %fusion.113 = (bf16[5,5,192,64]{3,2,1,0:T(8,128)(2,1)S(1)}, bf16[5,5,192,64]{3,2,1,0:T(8,128)(2,1)S(1)}, bf16[5,5,192,64]{3,2,1,0:T(8,128)(2,1)S(1)}, bf16[5,5,192,64]{3,2,1,0:T(8,128)(2,1)S(1)}) fusion(bf16[5,5,256,512]{3,2,1,0:T(8,128)(2,1)} %get-tuple-element.309), kind=kLoop, calls=%fused_computation.257 | loop fusion | bytes 4915200 | tf_op jit(solution)/shard_map/while/body/eval_jaxpr/cond/branch_3_fun/slice | solution.py:37
  261.4 4.2 %collective-permute-done.2 = bf16[16,32,128]{2,1,0:T(8,128)(2,1)} collective-permute-done((bf16[16,32,128]{2,1,0:T(8,128)(2,1)S(1)}, bf16[16,32,128]{2,1,0:T(8,128)(2,1)}, u32[]{:S(2)}, u32[]{:S(2)}) %collective-permute-start.2) | collective-permute-done | bytes 131104 | tf_op jit(solution)/shard_map/while/body/eval_jaxpr/ppermute | solution.py:29
  (132 shorter events, 67.2 us)
Async XLA Ops:
  7.2 7.8 %collective-permute-start = (bf16[2,32,256]{2,1,0:T(8,128)(2,1)S(1)}, bf16[2,32,256]{2,1,0:T(8,128)(2,1)S(1)}, u32[]{:S(2)}, u32[]{:S(2)}) collective-permute-start(bf16[2,32,256]{2,1,0:T(8,128)(2,1)S(1)} %get-tuple-element.505), channel_id=1, source_target_pairs={{1,0},{2,1},{3,2},{4,3},{5,4},{6,5},{7,6},{8,7},{9,8},{10,9},{11,1... | collective-permute-start | bytes 98312 | tf_op jit(solution)/shard_map/while/body/eval_jaxpr/ppermute | solution.py:17
  11.1 8.6 %collective-permute-start.1 = (bf16[2,32,256]{2,1,0:T(8,128)(2,1)S(1)}, bf16[2,32,256]{2,1,0:T(8,128)(2,1)S(1)}, u32[]{:S(2)}, u32[]{:S(2)}) collective-permute-start(bf16[2,32,256]{2,1,0:T(8,128)(2,1)S(1)} %get-tuple-element.506), channel_id=1, source_target_pairs={{0,1},{1,2},{2,3},{3,4},{4,5},{5,6},{6,7},{7,8},{8,9},{9,10},{10,1... | collective-permute-start | bytes 98312 | tf_op jit(solution)/shard_map/while/body/eval_jaxpr/ppermute | solution.py:16
  19.8 7.0 %collective-permute-start.2 = (bf16[16,32,128]{2,1,0:T(8,128)(2,1)S(1)}, bf16[16,32,128]{2,1,0:T(8,128)(2,1)}, u32[]{:S(2)}, u32[]{:S(2)}) collective-permute-start(bf16[16,32,128]{2,1,0:T(8,128)(2,1)S(1)} %get-tuple-element.507), channel_id=1, source_target_pairs={{0,64},{64,128},{128,192},{1,65},{65,129},{129,193},{2,66},{66,130... | collective-permute-start | bytes 393224 | tf_op jit(solution)/shard_map/while/body/eval_jaxpr/ppermute | solution.py:29
  28.7 6.3 %collective-permute-start = (bf16[2,32,256]{2,1,0:T(8,128)(2,1)S(1)}, bf16[2,32,256]{2,1,0:T(8,128)(2,1)S(1)}, u32[]{:S(2)}, u32[]{:S(2)}) collective-permute-start(bf16[2,32,256]{2,1,0:T(8,128)(2,1)S(1)} %get-tuple-element.505), channel_id=1, source_target_pairs={{1,0},{2,1},{3,2},{4,3},{5,4},{6,5},{7,6},{8,7},{9,8},{10,9},{11,1... | collective-permute-start | bytes 98312 | tf_op jit(solution)/shard_map/while/body/eval_jaxpr/ppermute | solution.py:17
  30.6 8.6 %collective-permute-start.1 = (bf16[2,32,256]{2,1,0:T(8,128)(2,1)S(1)}, bf16[2,32,256]{2,1,0:T(8,128)(2,1)S(1)}, u32[]{:S(2)}, u32[]{:S(2)}) collective-permute-start(bf16[2,32,256]{2,1,0:T(8,128)(2,1)S(1)} %get-tuple-element.506), channel_id=1, source_target_pairs={{0,1},{1,2},{2,3},{3,4},{4,5},{5,6},{6,7},{7,8},{8,9},{9,10},{10,1... | collective-permute-start | bytes 98312 | tf_op jit(solution)/shard_map/while/body/eval_jaxpr/ppermute | solution.py:16
  39.3 7.0 %collective-permute-start.2 = (bf16[16,32,128]{2,1,0:T(8,128)(2,1)S(1)}, bf16[16,32,128]{2,1,0:T(8,128)(2,1)}, u32[]{:S(2)}, u32[]{:S(2)}) collective-permute-start(bf16[16,32,128]{2,1,0:T(8,128)(2,1)S(1)} %get-tuple-element.507), channel_id=1, source_target_pairs={{0,64},{64,128},{128,192},{1,65},{65,129},{129,193},{2,66},{66,130... | collective-permute-start | bytes 393224 | tf_op jit(solution)/shard_map/while/body/eval_jaxpr/ppermute | solution.py:29
  48.2 6.3 %collective-permute-start = (bf16[2,32,256]{2,1,0:T(8,128)(2,1)S(1)}, bf16[2,32,256]{2,1,0:T(8,128)(2,1)S(1)}, u32[]{:S(2)}, u32[]{:S(2)}) collective-permute-start(bf16[2,32,256]{2,1,0:T(8,128)(2,1)S(1)} %get-tuple-element.505), channel_id=1, source_target_pairs={{1,0},{2,1},{3,2},{4,3},{5,4},{6,5},{7,6},{8,7},{9,8},{10,9},{11,1... | collective-permute-start | bytes 98312 | tf_op jit(solution)/shard_map/while/body/eval_jaxpr/ppermute | solution.py:17
  50.2 8.6 %collective-permute-start.1 = (bf16[2,32,256]{2,1,0:T(8,128)(2,1)S(1)}, bf16[2,32,256]{2,1,0:T(8,128)(2,1)S(1)}, u32[]{:S(2)}, u32[]{:S(2)}) collective-permute-start(bf16[2,32,256]{2,1,0:T(8,128)(2,1)S(1)} %get-tuple-element.506), channel_id=1, source_target_pairs={{0,1},{1,2},{2,3},{3,4},{4,5},{5,6},{6,7},{7,8},{8,9},{9,10},{10,1... | collective-permute-start | bytes 98312 | tf_op jit(solution)/shard_map/while/body/eval_jaxpr/ppermute | solution.py:16
  58.9 41.1 %collective-permute-start.2 = (bf16[16,32,128]{2,1,0:T(8,128)(2,1)S(1)}, bf16[16,32,128]{2,1,0:T(8,128)(2,1)}, u32[]{:S(2)}, u32[]{:S(2)}) collective-permute-start(bf16[16,32,128]{2,1,0:T(8,128)(2,1)S(1)} %get-tuple-element.507), channel_id=1, source_target_pairs={{0,64},{64,128},{128,192},{1,65},{65,129},{129,193},{2,66},{66,130... | collective-permute-start | bytes 393224 | tf_op jit(solution)/shard_map/while/body/eval_jaxpr/ppermute | solution.py:29
  101.9 6.3 %collective-permute-start = (bf16[2,32,256]{2,1,0:T(8,128)(2,1)S(1)}, bf16[2,32,256]{2,1,0:T(8,128)(2,1)S(1)}, u32[]{:S(2)}, u32[]{:S(2)}) collective-permute-start(bf16[2,32,256]{2,1,0:T(8,128)(2,1)S(1)} %get-tuple-element.505), channel_id=1, source_target_pairs={{1,0},{2,1},{3,2},{4,3},{5,4},{6,5},{7,6},{8,7},{9,8},{10,9},{11,1... | collective-permute-start | bytes 98312 | tf_op jit(solution)/shard_map/while/body/eval_jaxpr/ppermute | solution.py:17
  103.8 8.6 %collective-permute-start.1 = (bf16[2,32,256]{2,1,0:T(8,128)(2,1)S(1)}, bf16[2,32,256]{2,1,0:T(8,128)(2,1)S(1)}, u32[]{:S(2)}, u32[]{:S(2)}) collective-permute-start(bf16[2,32,256]{2,1,0:T(8,128)(2,1)S(1)} %get-tuple-element.506), channel_id=1, source_target_pairs={{0,1},{1,2},{2,3},{3,4},{4,5},{5,6},{6,7},{7,8},{8,9},{9,10},{10,1... | collective-permute-start | bytes 98312 | tf_op jit(solution)/shard_map/while/body/eval_jaxpr/ppermute | solution.py:16
  127.8 1.7 copy-start.6
  127.9 2.4 copy-start.2
  133.1 8.7 %collective-permute-start.2 = (bf16[16,32,128]{2,1,0:T(8,128)(2,1)S(1)}, bf16[16,32,128]{2,1,0:T(8,128)(2,1)}, u32[]{:S(2)}, u32[]{:S(2)}) collective-permute-start(bf16[16,32,128]{2,1,0:T(8,128)(2,1)S(1)} %get-tuple-element.507), channel_id=1, source_target_pairs={{0,64},{64,128},{128,192},{1,65},{65,129},{129,193},{2,66},{66,130... | collective-permute-start | bytes 393224 | tf_op jit(solution)/shard_map/while/body/eval_jaxpr/ppermute | solution.py:29
  143.8 6.3 %collective-permute-start = (bf16[2,32,256]{2,1,0:T(8,128)(2,1)S(1)}, bf16[2,32,256]{2,1,0:T(8,128)(2,1)S(1)}, u32[]{:S(2)}, u32[]{:S(2)}) collective-permute-start(bf16[2,32,256]{2,1,0:T(8,128)(2,1)S(1)} %get-tuple-element.505), channel_id=1, source_target_pairs={{1,0},{2,1},{3,2},{4,3},{5,4},{6,5},{7,6},{8,7},{9,8},{10,9},{11,1... | collective-permute-start | bytes 98312 | tf_op jit(solution)/shard_map/while/body/eval_jaxpr/ppermute | solution.py:17
  145.7 8.6 %collective-permute-start.1 = (bf16[2,32,256]{2,1,0:T(8,128)(2,1)S(1)}, bf16[2,32,256]{2,1,0:T(8,128)(2,1)S(1)}, u32[]{:S(2)}, u32[]{:S(2)}) collective-permute-start(bf16[2,32,256]{2,1,0:T(8,128)(2,1)S(1)} %get-tuple-element.506), channel_id=1, source_target_pairs={{0,1},{1,2},{2,3},{3,4},{4,5},{5,6},{6,7},{7,8},{8,9},{9,10},{10,1... | collective-permute-start | bytes 98312 | tf_op jit(solution)/shard_map/while/body/eval_jaxpr/ppermute | solution.py:16
  169.7 1.7 copy-start.6
  169.7 2.4 copy-start.2
  174.9 8.7 %collective-permute-start.2 = (bf16[16,32,128]{2,1,0:T(8,128)(2,1)S(1)}, bf16[16,32,128]{2,1,0:T(8,128)(2,1)}, u32[]{:S(2)}, u32[]{:S(2)}) collective-permute-start(bf16[16,32,128]{2,1,0:T(8,128)(2,1)S(1)} %get-tuple-element.507), channel_id=1, source_target_pairs={{0,64},{64,128},{128,192},{1,65},{65,129},{129,193},{2,66},{66,130... | collective-permute-start | bytes 393224 | tf_op jit(solution)/shard_map/while/body/eval_jaxpr/ppermute | solution.py:29
  185.6 6.3 %collective-permute-start = (bf16[2,32,256]{2,1,0:T(8,128)(2,1)S(1)}, bf16[2,32,256]{2,1,0:T(8,128)(2,1)S(1)}, u32[]{:S(2)}, u32[]{:S(2)}) collective-permute-start(bf16[2,32,256]{2,1,0:T(8,128)(2,1)S(1)} %get-tuple-element.505), channel_id=1, source_target_pairs={{1,0},{2,1},{3,2},{4,3},{5,4},{6,5},{7,6},{8,7},{9,8},{10,9},{11,1... | collective-permute-start | bytes 98312 | tf_op jit(solution)/shard_map/while/body/eval_jaxpr/ppermute | solution.py:17
  187.5 8.6 %collective-permute-start.1 = (bf16[2,32,256]{2,1,0:T(8,128)(2,1)S(1)}, bf16[2,32,256]{2,1,0:T(8,128)(2,1)S(1)}, u32[]{:S(2)}, u32[]{:S(2)}) collective-permute-start(bf16[2,32,256]{2,1,0:T(8,128)(2,1)S(1)} %get-tuple-element.506), channel_id=1, source_target_pairs={{0,1},{1,2},{2,3},{3,4},{4,5},{5,6},{6,7},{7,8},{8,9},{9,10},{10,1... | collective-permute-start | bytes 98312 | tf_op jit(solution)/shard_map/while/body/eval_jaxpr/ppermute | solution.py:16
  211.5 1.7 copy-start.6
  211.5 2.4 copy-start.2
  216.8 8.7 %collective-permute-start.2 = (bf16[16,32,128]{2,1,0:T(8,128)(2,1)S(1)}, bf16[16,32,128]{2,1,0:T(8,128)(2,1)}, u32[]{:S(2)}, u32[]{:S(2)}) collective-permute-start(bf16[16,32,128]{2,1,0:T(8,128)(2,1)S(1)} %get-tuple-element.507), channel_id=1, source_target_pairs={{0,64},{64,128},{128,192},{1,65},{65,129},{129,193},{2,66},{66,130... | collective-permute-start | bytes 393224 | tf_op jit(solution)/shard_map/while/body/eval_jaxpr/ppermute | solution.py:29
  227.5 6.3 %collective-permute-start = (bf16[2,32,256]{2,1,0:T(8,128)(2,1)S(1)}, bf16[2,32,256]{2,1,0:T(8,128)(2,1)S(1)}, u32[]{:S(2)}, u32[]{:S(2)}) collective-permute-start(bf16[2,32,256]{2,1,0:T(8,128)(2,1)S(1)} %get-tuple-element.505), channel_id=1, source_target_pairs={{1,0},{2,1},{3,2},{4,3},{5,4},{6,5},{7,6},{8,7},{9,8},{10,9},{11,1... | collective-permute-start | bytes 98312 | tf_op jit(solution)/shard_map/while/body/eval_jaxpr/ppermute | solution.py:17
  229.4 8.6 %collective-permute-start.1 = (bf16[2,32,256]{2,1,0:T(8,128)(2,1)S(1)}, bf16[2,32,256]{2,1,0:T(8,128)(2,1)S(1)}, u32[]{:S(2)}, u32[]{:S(2)}) collective-permute-start(bf16[2,32,256]{2,1,0:T(8,128)(2,1)S(1)} %get-tuple-element.506), channel_id=1, source_target_pairs={{0,1},{1,2},{2,3},{3,4},{4,5},{5,6},{6,7},{7,8},{8,9},{9,10},{10,1... | collective-permute-start | bytes 98312 | tf_op jit(solution)/shard_map/while/body/eval_jaxpr/ppermute | solution.py:16
  253.4 1.7 copy-start.6
  253.4 2.4 copy-start.2
  258.6 7.0 %collective-permute-start.2 = (bf16[16,32,128]{2,1,0:T(8,128)(2,1)S(1)}, bf16[16,32,128]{2,1,0:T(8,128)(2,1)}, u32[]{:S(2)}, u32[]{:S(2)}) collective-permute-start(bf16[16,32,128]{2,1,0:T(8,128)(2,1)S(1)} %get-tuple-element.507), channel_id=1, source_target_pairs={{0,64},{64,128},{128,192},{1,65},{65,129},{129,193},{2,66},{66,130... | collective-permute-start | bytes 393224 | tf_op jit(solution)/shard_map/while/body/eval_jaxpr/ppermute | solution.py:29
where the time goes:
time: 271 us; the launch traced here: 266 us
  waiting for transfers between devices  99.1 us (37%)
  local copies, waits for them, and re-layouts  92.4 us (34%)
  starting transfers between devices  40.8 us (15%)
  other arithmetic  25.6 us (9%)
  matrix products  5.79 us (2%)
    ppermute x7, waiting for transfers between devices, shifted(): return lax.ppermute(x, axis, pairs)  69.1 us
    concatenate x4, local copies, waits for them, and re-layouts, cell_update(): patches = jnp.concatenate(windows, axis=-1).reshape(rows * cols, -1)  40.1 us
    ppermute x7, waiting for transfers between devices, with_halo(): before = lax.ppermute(last, axis, up)  30 us
    ppermute x7, starting transfers between devices, with_halo(): before = lax.ppermute(last, axis, up)  16.4 us
    ppermute x7, starting transfers between devices, with_halo(): after = lax.ppermute(initial, axis, down)  15.4 us
    slice x4, local copies, waits for them, and re-layouts, layer_kernel(): rows_cut[..., k * wide:k * wide + hidden_width]  11.3 us
    slice x8, local copies, waits for them, and re-layouts, cell_update(): broad[first:first + rows, second:second + cols, :]  10.1 us
    ppermute x7, starting transfers between devices, shifted(): return lax.ppermute(x, axis, pairs)  9.04 us
  transfers between devices with their start and end apart: 21, of which 14 were waited for; matrix products, arithmetic and copies ran while one was open for 9% of the time, Pallas kernels for 0%

commit v1 on v0

v1 whole, which is shorter than its diff:
```python
import functools

import jax
import jax.numpy as jnp
from jax import lax
from jax.experimental import pallas as pl
from jax.experimental.pallas import tpu as pltpu
from jax.sharding import PartitionSpec as P

MESH = pl.DeviceIdType.MESH
F32 = jnp.float32
BF16 = jnp.bfloat16
KER = 5
HALO = 2


def lane_halves(low, high):
    lane = lax.broadcasted_iota(jnp.int32, low.shape, low.ndim - 1)
    return jnp.where(lane < 64, low, pltpu.roll(high, 64, low.ndim - 1))


def put_shifts(value, dst):
    rows, cols, chans = value.shape
    flat = value.reshape(rows * cols, chans)
    col = lax.broadcasted_iota(jnp.int32, (rows, cols, chans), 1).reshape(rows * cols, chans)
    for b in range(KER):
        by = b - HALO
        if by == 0:
            moved = flat
        else:
            moved = pltpu.roll(flat, (-by) % (rows * cols), 0)
            inside = (col < cols - by) if by > 0 else (col >= -by)
            moved = jnp.where(inside, moved, 0.0)
        dst[:, :, 128 * b : 128 * (b + 1)] = moved.astype(BF16).reshape(rows, cols, chans)


def conv(buf, weights, rows, cols, step, first=0, count=None):
    taps = weights.shape[0]
    lhs = jnp.concatenate(
        [buf[step * a : step * a + rows].reshape(rows * cols, KER * 128) for a in range(taps)], axis=1
    )
    n = weights.shape[-1]
    return jnp.dot(lhs, weights[...].reshape(taps * KER * 128, n), preferred_element_type=F32)


def sigmoid(x):
    return 0.5 * jnp.tanh(0.5 * x) + 0.5


def kernel(
    segments, spaces,
    frames, hprev, cprev, kern, bias_in,
    hout, cout,
    wx, wh, w3, wxc, w3c, bias, biasc,
    fraw, hraw, xraw, shift_a, shift_b, acc, cell, cnew, hnew,
    w_sem, in_sem, halo_send, halo_recv, x_send, x_recv, out_sem,
):
    seg = lax.axis_index("segment")
    sp = lax.axis_index("space")
    batches, rows, cols = (frames.shape[0], frames.shape[1], frames.shape[2])
    m_rows = rows * cols
    top, bottom = (sp > 0, sp < spaces - 1)
    above, below = (lax.rem(sp + spaces - 1, spaces), lax.rem(sp + 1, spaces))
    nxt, prv = (lax.rem(seg + 1, segments), lax.rem(seg + segments - 1, segments))

    barrier = pltpu.get_barrier_semaphore()
    others = [(seg, above), (seg, below)]
    others += [(k, s) for k in (nxt, prv) for s in (above, sp, below)]
    for other in others:
        pl.semaphore_signal(barrier, inc=1, device_id=other, device_id_type=MESH)

    def remote(src, dst, send, recv, k, s):
        return pltpu.make_async_remote_copy(
            src_ref=src, dst_ref=dst, send_sem=send, recv_sem=recv, device_id=(k, s), device_id_type=MESH
        )

    def local(src, dst, sem):
        return pltpu.make_async_copy(src, dst, sem)

    def weight_copies(layer):
        if layer == 0:
            for a in range(KER):
                yield local(kern.at[0, a, :, 0:64], wx.at[a, :, 0:64], w_sem.at[a])
                yield local(kern.at[0, a, :, 128:192], wx.at[a, :, 64:128], w_sem.at[KER + a])
        elif layer == 1:
            for a in range(KER):
                yield local(kern.at[0, a, :, 128:256], wh.at[a], w_sem.at[a])
            for a in range(KER):
                half = 64 * (a % 2)
                yield local(kern.at[0, a, :, 0:64], w3.at[a // 2, :, half : half + 64], w_sem.at[KER + a])
        elif layer == 2:
            for a in range(KER):
                yield local(kern.at[0, a, :, 128:256], wh.at[a], w_sem.at[a])
            for a in range(KER):
                yield local(kern.at[0, a, :, 0:128], wx.at[a], w_sem.at[KER + a])
        else:
            for a in range(KER):
                half = 64 * (a % 2)
                yield local(kern.at[0, a, :, 128:192], w3.at[a // 2, :, half : half + 64], w_sem.at[a])
            for a in range(KER):
                yield local(kern.at[0, a, :, 0:128], wx.at[a], w_sem.at[KER + a])

    state_in = [
        local(hprev.at[0], hraw.at[:, HALO : HALO + rows], in_sem.at[0]),
        local(bias_in, bias, in_sem.at[1]),
        local(cprev.at[0], cell, in_sem.at[2]),
    ]
    frames_in = local(frames, fraw.at[:, HALO : HALO + rows], in_sem.at[3])
    state_in[0].start()
    pl.when(seg == 0)(frames_in.start)
    for layer in range(4):

        @pl.when(seg == layer)
        def _(layer=layer):
            for copy in weight_copies(layer):
                copy.start()

    state_in[1].start()
    state_in[2].start()

    def edges(src, dst, index):
        up = remote(src.at[:, 0:HALO], dst.at[:, HALO + rows :], halo_send.at[index], halo_recv.at[index], seg, above)
        down = remote(
            src.at[:, rows - HALO :], dst.at[:, 0:HALO], halo_send.at[index + 1], halo_recv.at[index + 1], seg, below
        )
        return (up, down)

    pl.semaphore_wait(barrier, len(others))
    h_up, h_down = edges(hprev.at[0], hraw, 0)
    f_up, f_down = edges(frames, fraw, 2)
    pl.when(top)(h_up.start)
    pl.when(bottom)(h_down.start)
    pl.when(jnp.logical_and(seg == 0, top))(f_up.start)
    pl.when(jnp.logical_and(seg == 0, bottom))(f_down.start)

    @pl.when(sp == 0)
    def _():
        hraw[:, 0:HALO] = jnp.zeros((batches, HALO, cols, 128), BF16)
        xraw[:, 0:HALO] = jnp.zeros((batches, HALO, cols, 128), BF16)
        fraw[:, 0:HALO] = jnp.zeros((batches, HALO, cols, 64), BF16)

    @pl.when(sp == spaces - 1)
    def _():
        hraw[:, HALO + rows :] = jnp.zeros((batches, HALO, cols, 128), BF16)
        xraw[:, HALO + rows :] = jnp.zeros((batches, HALO, cols, 128), BF16)
        fraw[:, HALO + rows :] = jnp.zeros((batches, HALO, cols, 64), BF16)

    def sends(m):
        return (
            remote(hnew.at[m], xraw.at[m, HALO : HALO + rows], x_send.at[m, 0], x_recv.at[m, 0], nxt, sp),
            remote(
                hnew.at[m, 0:HALO], xraw.at[m, HALO + rows :], x_send.at[m, 1], x_recv.at[m, 1], nxt, above
            ),
            remote(
                hnew.at[m, rows - HALO :], xraw.at[m, 0:HALO], x_send.at[m, 2], x_recv.at[m, 2], nxt, below
            ),
        )

    def results(m):
        return (
            local(hnew.at[m], hout.at[0, m], out_sem.at[m, 0]),
            local(cnew.at[m], cout.at[0, m], out_sem.at[m, 1]),
        )

    def wait_x(m):
        main, up, down = sends(m)
        main.wait_recv()
        pl.when(bottom)(up.wait_recv)
        pl.when(top)(down.wait_recv)

    def wait_h(extra):
        state_in[0].wait()
        pl.when(bottom)(h_up.wait_recv)
        pl.when(top)(h_down.wait_recv)
        if extra:
            frames_in.wait()
            pl.when(bottom)(f_up.wait_recv)
            pl.when(top)(f_down.wait_recv)

    def padded(ref, m):
        return ref[m].astype(F32)

    def row_pairs(ref, m):
        low = ref[m].astype(F32)
        high = jnp.concatenate([low[1:], jnp.zeros_like(low[:1])], axis=0)
        return lane_halves(low, high)

    def compact(src, dst, taps):
        for a in range(taps):
            for b in range(KER):
                part = [src[a, b, :, 128 * g : 128 * (g + 1)].astype(F32) for g in range(4)]
                dst[a, b, :, 0:128] = lane_halves(part[1], part[0]).astype(BF16)
                dst[a, b, :, 128:256] = lane_halves(part[3], part[2]).astype(BF16)

    def compact_bias():
        part = [bias[:, 128 * g : 128 * (g + 1)] for g in range(4)]
        lane = lax.broadcasted_iota(jnp.int32, (1, 128), 1)
        swap = lambda x: jnp.concatenate([x[:, 64:], x[:, :64]], axis=1)
        biasc[:, 0:128] = jnp.where(lane < 64, part[1], swap(part[0]))
        biasc[:, 128:256] = jnp.where(lane < 64, part[3], swap(part[2]))

    piece = 2

    def finish(m, narrow):
        for r in range(0, rows, piece):
            at = slice(r * cols, (r + piece) * cols)
            old = cell[m, r : r + piece].reshape(piece * cols, 128)
            if narrow:
                fi = sigmoid(acc[m, at, 0:128] + biasc[:, 0:128])
                og = acc[m, at, 128:256] + biasc[:, 128:256]
                gained = pltpu.roll(fi * jnp.tanh(og), 64, 1)
                new = fi * old + gained
                out = sigmoid(og) * jnp.tanh(new)
                lane = lax.broadcasted_iota(jnp.int32, new.shape, 1)
                new = jnp.where(lane < 64, new, 0.0)
                out = jnp.where(lane < 64, out, 0.0)
            else:
                gate = [acc[m, at, 128 * g : 128 * (g + 1)] + bias[:, 128 * g : 128 * (g + 1)] for g in range(4)]
                new = sigmoid(gate[1]) * old + sigmoid(gate[0]) * jnp.tanh(gate[2])
                out = sigmoid(gate[3]) * jnp.tanh(new)
            cnew[m, r : r + piece] = new.reshape(piece, cols, 128)
            hnew[m, r : r + piece] = out.astype(BF16).reshape(piece, cols, 128)

    def emit(m, layer):
        if layer < 3:
            main, up, down = sends(m)
            main.start()
            pl.when(top)(up.start)
            pl.when(bottom)(down.start)
        for copy in results(m):
            copy.start()

    def wait_small():
        state_in[1].wait()
        state_in[2].wait()

    @pl.when(seg == 0)
    def _():
        for copy in weight_copies(0):
            copy.wait()
        compact(wx, wxc, KER)
        wait_small()
        compact_bias()
        wait_h(True)

        @pl.loop(0, batches)
        def _(m):
            f = fraw[m].astype(F32)
            f = jnp.concatenate([f, jnp.zeros_like(f)], axis=-1)
            put_shifts(lane_halves(f, hraw[m].astype(F32)), shift_a)
            acc[m, :, 0:256] = conv(shift_a, wxc, rows, cols, 1)
            finish(m, True)
            emit(m, 0)

    def wide(layer, x_first):
        copies = list(weight_copies(layer))
        for copy in copies[:KER]:
            copy.wait()
        wait_h(False)

        def hidden(m):
            put_shifts(padded(hraw, m), shift_a)
            acc[m] = conv(shift_a, wh, rows, cols, 1)

        def incoming(m):
            wait_x(m)
            if layer == 1:
                put_shifts(row_pairs(xraw, m), shift_b)
                acc[m] += conv(shift_b, w3, rows, cols, 2)
            else:
                put_shifts(padded(xraw, m), shift_b)
                acc[m] += conv(shift_b, wx, rows, cols, 1)
            finish(m, False)
            emit(m, layer)

        pl.loop(0, x_first)(hidden)
        for copy in copies[KER:]:
            copy.wait()
        wait_small()

        @pl.loop(0, batches)
        def _(m):
            incoming(m)
            pl.when(m + x_first < batches)(lambda: hidden(m + x_first))

    @pl.when(seg == 1)
    def _():
        w3[2, :, 64:128] = jnp.zeros((KER, 64, 512), BF16)
        wide(1, 2)

    @pl.when(seg == 2)
    def _():
        wide(2, 3)

    @pl.when(seg == 3)
    def _():
        w3[2, :, 64:128] = jnp.zeros((KER, 64, 512), BF16)
        copies = list(weight_copies(3))
        for copy in copies[:KER]:
            copy.wait()
        compact(w3, w3c, 3)
        wait_h(False)

        @pl.loop(0, batches)
        def _(m):
            put_shifts(row_pairs(hraw, m), shift_a)
            acc[m, :, 0:256] = conv(shift_a, w3c, rows, cols, 2)

        for copy in copies[KER:]:
            copy.wait()
        compact(wx, wxc, KER)
        wait_small()
        compact_bias()

        @pl.loop(0, batches)
        def _(m):
            wait_x(m)
            put_shifts(padded(xraw, m), shift_b)
            acc[m, :, 0:256] += conv(shift_b, wxc, rows, cols, 1)
            finish(m, True)
            emit(m, 3)

    @pl.loop(0, batches)
    def _(m):
        for copy in results(m):
            copy.wait()

        @pl.when(seg < 3)
        def _():
            main, up, down = sends(m)
            main.wait_send()
            pl.when(top)(up.wait_send)
            pl.when(bottom)(down.wait_send)

    pl.when(top)(h_up.wait_send)
    pl.when(bottom)(h_down.wait_send)
    pl.when(jnp.logical_and(seg == 0, top))(f_up.wait_send)
    pl.when(jnp.logical_and(seg == 0, bottom))(f_down.wait_send)


def on_device(frames, hidden_prev, cell_prev, kernels, biases):
    segments, spaces = (lax.axis_size("segment"), lax.axis_size("space"))
    batches, rows, cols, narrow = frames.shape
    wide = hidden_prev.shape[-1]
    tall = rows + 2 * HALO
    anywhere = pl.BlockSpec(memory_space=pl.ANY)
    vmem, dma = (pltpu.VMEM, pltpu.SemaphoreType.DMA)
    return pl.pallas_call(
        functools.partial(kernel, segments, spaces),
        out_shape=(
            jax.ShapeDtypeStruct(hidden_prev.shape, BF16),
            jax.ShapeDtypeStruct(cell_prev.shape, F32),
        ),
        in_specs=[anywhere] * 5,
        out_specs=[anywhere] * 2,
        scratch_shapes=[
            vmem((KER, KER, 128, 512), BF16),
            vmem((KER, KER, 128, 512), BF16),
            vmem((3, KER, 128, 512), BF16),
            vmem((KER, KER, 128, 256), BF16),
            vmem((3, KER, 128, 256), BF16),
            vmem((1, 512), F32),
            vmem((1, 256), F32),
            vmem((batches, tall, cols, narrow), BF16),
            vmem((batches, tall, cols, wide), BF16),
            vmem((batches, tall, cols, wide), BF16),
            vmem((tall, cols, KER * wide), BF16),
            vmem((tall, cols, KER * wide), BF16),
            vmem((batches, rows * cols, 4 * wide), F32),
            vmem((batches, rows, cols, wide), F32),
            vmem((batches, rows, cols, wide), F32),
            vmem((batches, rows, cols, wide), BF16),
            dma((2 * KER,)),
            dma((4,)),
            dma((4,)),
            dma((4,)),
            dma((batches, 3)),
            dma((batches, 3)),
            dma((batches, 2)),
        ],
        compiler_params=pltpu.CompilerParams(
            collective_id=0, has_side_effects=True, vmem_limit_bytes=56 * 2**20
        ),
        name="step",
    )(frames, hidden_prev, cell_prev, kernels, biases)


def solution(mesh):
    return jax.shard_map(
        on_device,
        mesh=mesh,
        in_specs=(
            P(None, "space", None, None),
            P("segment", None, "space", None, None),
            P("segment", None, "space", None, None),
            P("segment", None, None, None, None),
            P("segment", None),
        ),
        out_specs=(
            P("segment", None, "space", None, None),
            P("segment", None, "space", None, None),
        ),
        check_vma=False,
    )
```

time: 271 us -> 50.9 us (0.19)
  the two profiles are of different devices: /device:TPU:134 before, /device:TPU:7 now
where the time goes in v1:
time: 50.9 us; the launch traced here: 50.8 us
  Pallas kernels  46 us (90%)
  local copies, waits for them, and re-layouts  4.13 us (8%)
  between operations  0.64 us (1%)
    pallas_call x1, Pallas kernels, on_device(): pl.pallas_call(functools.partial(kernel, segments, spaces), out_shape=(ja...  46 us
    unnamed x2, local copies, waits for them, and re-layouts  4.13 us

profile of v1, /device:TPU:7, one launch (start us, length us, event | category | flops | bytes accessed | tf_op | source)
XLA Modules:
  0.0 50.8 jit_solution(12695458238203570159)
XLA Ops:
  0.6 46.0 %step.1 = (bf16[1,4,16,32,128]{4,3,2,1,0:T(8,128)(2,1)}, f32[1,4,16,32,128]{4,3,2,1,0:T(8,128)}) custom-call(bf16[4,16,32,64]{3,2,1,0:T(8,128)(2,1)} %frames.1, bf16[1,4,16,32,128]{4,3,2,1,0:T(8,128)(2,1)} %hprev.1, f32[1,4,16,32,128]{4,3,2,1,0:T(8,128)} %cprev.1, bf16[1,5,5,256,512]{4,3,2,1,0:T(8,128)(2,1)} %kern.1, f32[1,512]{1,0:T(1,128)} %bias_in.1), custom_call_target="tpu_custom_call" | custom-call | tf_op jit(solution)/shard_map/step/pallas_call | solution.py:348
  46.6 1.9 %copy.9 = bf16[1,4,16,32,128]{4,3,2,1,0:T(8,128)(2,1)} copy(bf16[1,4,16,32,128]{4,3,2,1,0:T(8,128)(2,1)} %get-tuple-element.4) | data formatting | bytes 1048576
  48.5 2.3 %copy.10 = f32[1,4,16,32,128]{4,3,2,1,0:T(8,128)} copy(f32[1,4,16,32,128]{4,3,2,1,0:T(8,128)} %get-tuple-element.5) | data formatting | bytes 2097152
